TPU v7x, 32 devices: a whole 2x2x4 slice. The times are simulated.
32 devices in a mesh: groups: 2 (over y), tensor: 16 (over z, x, core).
Axes of the slice: x: 2, y: 2, z: 4, core: 2. Of those that a mesh axis runs over, the one named last changes fastest.
Arguments:
- token_ids: int32 [16, 4], P('tensor', 'groups'), parts along dimension 1, may hold values from 0 to 63
- lengths: int32 [4], P('groups'), parts along dimension 0, may hold values from 8 to 16, as said below
- embed_table: bfloat16 [64, 6144], replicated, may hold values from -6 to 6
- gain_attn: float32 [6144], replicated, may hold values from 0.1 to 1.9
- w_qkv: bfloat16 [6144, 18432], P(None, 'tensor'), may hold values from -0.078125 to 0.078125
- w_out: bfloat16 [6144, 6144], P(None, 'tensor'), may hold values from -0.078125 to 0.078125
- gain_first: float32 [6144], replicated, may hold values from 0.1 to 1.9
- gate_first: bfloat16 [6144, 16384], P(None, 'tensor'), may hold values from -0.078125 to 0.078125
- up_first: bfloat16 [6144, 16384], P(None, 'tensor'), may hold values from -0.078125 to 0.078125
- down_first: bfloat16 [16384, 6144], P('tensor'), may hold values from -0.09375 to 0.09375
- gain_second: float32 [6144], replicated, may hold values from 0.1 to 1.9
- gate_second: bfloat16 [6144, 16384], P(None, 'tensor'), may hold values from -0.078125 to 0.078125
- up_second: bfloat16 [6144, 16384], P(None, 'tensor'), may hold values from -0.078125 to 0.078125
- down_second: bfloat16 [16384, 6144], P('tensor'), may hold values from -0.09375 to 0.09375
Outputs:
- states: bfloat16 [16, 4, 6144], P('tensor', 'groups'), parts along dimension 1
There are 2 independent parts, one for each index of `groups`. A program takes and returns all parts, laid end to end along the dimension named above; an argument that names none is the same for every part. Nothing has to cross between parts.
Inputs may be any that keep to these rules, and one draw needn't show every extreme that they name: `lengths`: each micro-batch holds one protein of at least half of 16 positions; in every draw one micro-batch is full, 16 positions.
All inputs are finite; a program needn't handle non-finite values.
Results may differ from a plain program's by a relative error of at most 0.013.
Values may be sent and summed in bfloat16 or wider, within the bound.
No kernel may reach another device: no remote copies, remote signals or barrier semaphores. Data moves between devices by JAX's collectives and lax.ppermute only.
A program may use at most 192 MiB of HBM per device.

v0:
```python
import jax
import jax.numpy as jnp
from jax import lax
from jax.sharding import PartitionSpec as P

H = 48
HD = 128


def norm_rows(values, gain_vec):
    row_mean = jnp.mean(values, axis=-1, keepdims=True)
    centred = values - row_mean
    row_var = jnp.mean(centred * centred, axis=-1, keepdims=True)
    return (centred * lax.rsqrt(row_var + 1e-05) * gain_vec).astype(jnp.bfloat16)


def local_hidden(normed, gate_mat, up_mat):
    gated = jnp.einsum("pmd,dc->pmc", normed, gate_mat, preferred_element_type=jnp.float32)
    lifted = jnp.einsum("pmd,dc->pmc", normed, up_mat, preferred_element_type=jnp.float32)
    return (jax.nn.silu(gated) * lifted).astype(jnp.bfloat16)


def spread_rows(local_rows, row_fn):
    return row_fn(lax.all_gather(local_rows, "tensor", axis=0, tiled=True), jnp.int32(0))


def to_tokens(columns):
    return lax.all_to_all(columns, "tensor", split_axis=0, concat_axis=2, tiled=True)


def down_sum(hidden_all, down_mat):
    return lax.psum_scatter(
        jnp.einsum("pmc,cd->pmd", hidden_all, down_mat, preferred_element_type=jnp.float32),
        "tensor",
        scatter_dimension=0,
        tiled=True,
    )


def local(
    token_ids,
    lengths,
    embed_table,
    gain_attn,
    w_qkv,
    w_out,
    gain_first,
    gate_first,
    up_first,
    down_first,
    gain_second,
    gate_second,
    up_second,
    down_second,
):
    rows_here = token_ids.shape[0]
    micro_count = token_ids.shape[1]
    vocab_size = embed_table.shape[0]
    own_start = lax.axis_index("tensor") * rows_here
    onehot = (token_ids[:, :, None] == jnp.arange(vocab_size)[None, None, :]).astype(jnp.bfloat16)
    embedded = jnp.einsum("pmv,vd->pmd", onehot, embed_table, preferred_element_type=jnp.float32)
    normed_attn = norm_rows(embedded, gain_attn)

    def qkv_rows(row_piece, row_start):
        return jnp.einsum(
            "pmd,dc->pmc", row_piece, w_qkv, preferred_element_type=jnp.float32
        ).astype(jnp.bfloat16)

    projected = to_tokens(spread_rows(normed_attn, qkv_rows))
    feat_width = projected.shape[2] // 3
    queries = projected[..., :feat_width].reshape(rows_here, micro_count, H, HD)
    key_rows = projected[..., feat_width : 2 * feat_width]
    value_rows = projected[..., 2 * feat_width :]
    score_scale = HD ** (-0.5)
    key_piece = lax.all_gather(key_rows, "tensor", axis=0, tiled=True)
    value_piece = lax.all_gather(value_rows, "tensor", axis=0, tiled=True)
    piece_rows = key_piece.shape[0]
    key_heads = key_piece.reshape(piece_rows, micro_count, H, HD)
    value_heads = value_piece.reshape(piece_rows, micro_count, H, HD)
    scores = (
        jnp.einsum("pmhe,qmhe->pmhq", queries, key_heads, preferred_element_type=jnp.float32)
        * score_scale
    )
    positions = jnp.arange(piece_rows)
    live_keys = (positions[None, :] < lengths[:, None]).astype(jnp.float32)
    weights = jnp.exp(scores) * live_keys[None, :, None, :]
    denominator = jnp.sum(weights, axis=-1)
    numerator = jnp.einsum(
        "pmhq,qmhe->pmhe",
        weights.astype(jnp.bfloat16),
        value_heads,
        preferred_element_type=jnp.float32,
    )
    numerator, denominator = (numerator, denominator)
    attended = (
        (numerator / denominator[..., None])
        .reshape(rows_here, micro_count, feat_width)
        .astype(jnp.bfloat16)
    )

    def out_rows(row_piece, row_start):
        return jnp.einsum(
            "pmd,dc->pmc", row_piece, w_out, preferred_element_type=jnp.float32
        ).astype(jnp.bfloat16)

    after_attn = embedded + to_tokens(spread_rows(attended, out_rows)).astype(jnp.float32)

    def first_rows(row_piece, row_start):
        return local_hidden(row_piece, gate_first, up_first)

    hidden_first = spread_rows(norm_rows(after_attn, gain_first), first_rows)
    partial_all = jnp.einsum(
        "pmc,cd->pmd", hidden_first, down_first, preferred_element_type=jnp.float32
    )
    own_rows = lax.dynamic_slice_in_dim(partial_all, own_start, rows_here, 0) + after_attn
    partial_all = lax.dynamic_update_slice_in_dim(partial_all, own_rows, own_start, 0)
    first_all = lax.psum(partial_all, "tensor")
    after_first = lax.dynamic_slice_in_dim(first_all, own_start, rows_here, 0)
    hidden_second = local_hidden(norm_rows(first_all, gain_second), gate_second, up_second)
    after_second = after_first + down_sum(hidden_second, down_second)
    return after_second.astype(jnp.bfloat16)


def solution(mesh):
    return jax.shard_map(
        local,
        mesh=mesh,
        in_specs=(
            P("tensor", "groups"),
            P("groups"),
            P(),
            P(),
            P(None, "tensor"),
            P(None, "tensor"),
            P(),
            P(None, "tensor"),
            P(None, "tensor"),
            P("tensor", None),
            P(),
            P(None, "tensor"),
            P(None, "tensor"),
            P("tensor", None),
        ),
        out_specs=P("tensor", "groups", None),
        check_vma=False,
    )
```

profile of v0, /device:TPU:0, one launch (start us, length us, event | category | flops | bytes accessed | tf_op | source)
XLA Modules:
  0.0 383.6 jit_solution(4767694113768598177)
XLA Ops:
  6.5 1.1 copy-done
  7.7 1.0 fusion.79
  8.7 0.2 multiply_reduce_fusion.2
  9.0 0.8 fusion.64
  9.8 24.2 %all-gather.2 = bf16[16,2,6144]{2,1,0:T(2,128)(2,1)S(1)} all-gather(bf16[1,2,6144]{2,1,0:T(2,128)(2,1)S(1)} %fusion.64), channel_id=2, replica_groups=mesh['groups'=2,'tensor'=16] {'tensor'}, dimensions={0}, use_global_device_ids=true | all-gather | bytes 417792 | tf_op jit(solution)/shard_map/all_gather | solution.py:24
  34.0 7.6 %fusion.16 = bf16[16,2,1152]{2,0,1:T(8,128)(2,1)S(1)} fusion(bf16[6144,1152]{1,0:T(8,128)(2,1)} %param.18, bf16[16,2,6144]{2,1,0:T(2,128)(2,1)S(1)} %all-gather.2), kind=kOutput, calls=%fused_computation.16 | convolution fusion | flops 453021696 | bytes 14622720 | tf_op jit(solution)/shard_map/pmd,dc->pmc/dot_general | solution.py:65
  41.6 0.7 copy.49
  42.2 3.5 all-to-all-start
  45.8 0.1 compare_convert_fusion
  45.8 6.9 %all-to-all-done = bf16[16,2,1152]{2,1,0:T(2,128)(2,1)S(1)} async-done(((bf16[16,2,1152]{2,1,0:T(2,128)(2,1)}), bf16[16,2,1152]{2,1,0:T(2,128)(2,1)S(1)}, u32[]{:S(2)}, u32[]{:S(2)}) %all-to-all-start) | async-done | bytes 73760 | tf_op jit(solution)/shard_map/all_to_all | solution.py:28
  52.7 0.1 fusion.78
  52.8 18.8 %all_gather.17 = bf16[16,2,6144]{2,1,0:T(2,128)(2,1)S(1)} all-gather(bf16[1,2,6144]{2,1,0:T(2,128)(2,1)S(1)} %get-tuple-element.9), channel_id=1, replica_groups=mesh['groups'=2,'tensor'=16] {'tensor'}, dimensions={0}, use_global_device_ids=true | all-gather | bytes 417792 | tf_op jit(solution)/shard_map/all_gather | solution.py:75
  71.6 0.2 reshape.163
  71.8 0.3 fusion.40
  72.2 0.1 copy.61
  72.2 0.1 fusion.68
  72.3 0.1 copy.63
  72.4 19.6 %all_gather.16 = bf16[16,2,6144]{2,1,0:T(2,128)(2,1)S(1)} all-gather(bf16[1,2,6144]{2,1,0:T(2,128)(2,1)S(1)} %get-tuple-element.7), channel_id=1, replica_groups=mesh['groups'=2,'tensor'=16] {'tensor'}, dimensions={0}, use_global_device_ids=true | all-gather | bytes 417792 | tf_op jit(solution)/shard_map/all_gather | solution.py:76
  92.0 0.2 reshape.162
  92.3 0.2 fusion.38
  92.5 0.1 divide_convert_fusion
  92.7 19.0 %all_gather.18 = bf16[16,2,6144]{2,1,0:T(2,128)(2,1)S(1)} all-gather(bf16[1,2,6144]{2,1,0:T(2,128)(2,1)S(1)} %convert_element_type.75), channel_id=1, replica_groups=mesh['groups'=2,'tensor'=16] {'tensor'}, dimensions={0}, use_global_device_ids=true | all-gather | bytes 417792 | tf_op jit(solution)/shard_map/all_gather | solution.py:24
  111.6 3.1 fusion.35
  114.8 0.6 copy.51
  115.4 3.5 all-to-all-start.1
  118.9 0.0 all-reduce.4.cloned.1.call-start
  119.0 6.5 %all-to-all-done.1 = bf16[16,2,384]{2,1,0:T(2,128)(2,1)S(1)} async-done(((bf16[16,2,384]{2,1,0:T(2,128)(2,1)}), bf16[16,2,384]{2,1,0:T(2,128)(2,1)S(1)}, u32[]{:S(2)}, u32[]{:S(2)}) %all-to-all-start.1) | async-done | bytes 24608 | tf_op jit(solution)/shard_map/all_to_all | solution.py:28
  125.5 0.2 fusion.77
  125.7 0.2 multiply_reduce_fusion.1
  125.9 0.1 fusion.65
  126.0 18.6 %all-gather.3 = bf16[16,2,6144]{2,1,0:T(2,128)(2,1)S(1)} all-gather(bf16[1,2,6144]{2,1,0:T(2,128)(2,1)S(1)} %fusion.65), channel_id=3, replica_groups=mesh['groups'=2,'tensor'=16] {'tensor'}, dimensions={0}, use_global_device_ids=true | all-gather | bytes 417792 | tf_op jit(solution)/shard_map/all_gather | solution.py:24
  144.7 6.8 %fusion.12 = f32[16,2,1024]{2,0,1:T(8,128)S(1)} fusion(bf16[6144,1024]{1,0:T(8,128)(2,1)} %param.21, bf16[16,2,6144]{2,1,0:T(2,128)(2,1)S(1)} %all-gather.3), kind=kOutput, calls=%fused_computation.12 | convolution fusion | flops 402653184 | bytes 13107200 | tf_op jit(solution)/shard_map/pmd,dc->pmc/dot_general | solution.py:18
  151.5 12.6 %fusion.8 = f32[16,2,6144]{2,0,1:T(8,128)S(1)} fusion(bf16[1024,6144]{1,0:T(8,128)(2,1)} %param.23, bf16[6144,1024]{1,0:T(8,128)(2,1)} %param.22, bf16[16,2,6144]{2,1,0:T(2,128)(2,1)S(1)} %all-gather.3, f32[16,2,1024]{2,0,1:T(8,128)S(1)} %fusion.12), kind=kOutput, calls=%fused_computation.8 | convolution fusion | flops 805502976 | bytes 26476544 | tf_op jit(solution)/shard_map/pmc,cd->pmd/dot_general | solution.py:112
  164.1 0.6 copy.55
  164.8 0.9 copy-done.2
  165.7 0.0 all-reduce.4.cloned.1.call-update
  165.7 0.2 all-reduce.6.cloned.1.call-start
  165.9 91.0 %all-reduce.4.cloned.1.call-done = f32[16,2,6144]{2,1,0:T(2,128)} async-done(((f32[16,2,6144]{2,1,0:T(2,128)}), f32[16,2,6144]{2,1,0:T(2,128)}) %all-reduce.4.cloned.1.call-update) | async-done | bytes 786448 | tf_op jit(solution)/shard_map/psum | solution.py:117
  256.9 1.4 reduce_sum.68
  258.4 1.7 multiply_reduce_fusion
  260.1 1.7 multiply_convert_fusion
  261.7 6.9 %fusion.6 = f32[16,2,1024]{2,0,1:T(8,128)S(1)} fusion(bf16[6144,1024]{1,0:T(8,128)(2,1)} %param.25, bf16[16,2,6144]{2,1,0:T(2,128)(2,1)S(1)} %multiply_convert_fusion), kind=kOutput, calls=%fused_computation.6 | convolution fusion | flops 402653184 | bytes 13107200 | tf_op jit(solution)/shard_map/pmd,dc->pmc/dot_general | solution.py:18
  268.7 12.6 %fusion.2 = f32[16,2,6144]{2,0,1:T(8,128)S(1)} fusion(bf16[1024,6144]{1,0:T(8,128)(2,1)} %param.27, bf16[6144,1024]{1,0:T(8,128)(2,1)} %param.26, bf16[16,2,6144]{2,1,0:T(2,128)(2,1)S(1)} %multiply_convert_fusion, f32[16,2,1024]{2,0,1:T(8,128)S(1)} %fusion.6), kind=kOutput, calls=%fused_computation.2 | convolution fusion | flops 805502976 | bytes 26476544 | tf_op jit(solution)/shard_map/pmc,cd->pmd/dot_general | solution.py:33
  281.3 1.5 copy.58
  282.8 0.0 all-reduce.6.cloned.1.call-update
  282.8 0.6 dynamic-slice
  283.4 91.3 %all-reduce.6.cloned.1.call-done = f32[16,2,6144]{2,1,0:T(2,128)} async-done(((f32[16,2,6144]{2,1,0:T(2,128)}), f32[16,2,6144]{2,1,0:T(2,128)}) %all-reduce.6.cloned.1.call-update) | async-done | bytes 786448
  374.7 2.0 fusion.62
  (22 shorter events, 0.2 us)
Async XLA Ops:
  6.5 1.1 copy-start
  6.5 39.2 %copy-start.5 = (s32[2]{0:T(128)S(1)}, s32[2]{0:T(128)}, u32[]{:S(2)}) copy-start(s32[2]{0:T(128)} %param.15) | copy-start | bytes 28
  34.0 91.9 %copy-start.3 = (f32[6144]{0:T(1024)S(1)}, f32[6144]{0:T(1024)}, u32[]{:S(2)}) copy-start(f32[6144]{0:T(1024)} %param.20) | copy-start | bytes 73732
  42.2 10.5 %all-to-all-start = ((bf16[16,2,1152]{2,1,0:T(2,128)(2,1)}), bf16[16,2,1152]{2,1,0:T(2,128)(2,1)S(1)}, u32[]{:S(2)}, u32[]{:S(2)}) async-start(bf16[16,2,1152]{2,1,0:T(2,128)(2,1)} %copy.49), calls=%async_computation | async-start | bytes 147456 | tf_op jit(solution)/shard_map/all_to_all | solution.py:28
  115.4 10.0 %all-to-all-start.1 = ((bf16[16,2,384]{2,1,0:T(2,128)(2,1)}), bf16[16,2,384]{2,1,0:T(2,128)(2,1)S(1)}, u32[]{:S(2)}, u32[]{:S(2)}) async-start(bf16[16,2,384]{2,1,0:T(2,128)(2,1)} %copy.51), calls=%async_computation.1 | async-start | bytes 49152 | tf_op jit(solution)/shard_map/all_to_all | solution.py:28
  118.9 138.0 %all-reduce.4.cloned.1.call-start = ((), (), s32[]{:S(2)}) async-start(), calls=%async_computation.2 | async-start | bytes 1572864 | tf_op jit(solution)/shard_map/psum | solution.py:117
  151.5 108.6 %copy-start.4 = (f32[6144]{0:T(1024)S(1)}, f32[6144]{0:T(1024)}, u32[]{:S(2)}) copy-start(f32[6144]{0:T(1024)} %param.24) | copy-start | bytes 73732
  164.8 0.9 copy-start.2
  165.7 209.0 %all-reduce.6.cloned.1.call-start = ((), (), s32[]{:S(2)}) async-start(), calls=%async_computation.3 | async-start | bytes 1572864
  261.7 115.0 %copy-start.1 = (bf16[64,6144]{1,0:T(8,128)(2,1)S(1)}, bf16[64,6144]{1,0:T(8,128)(2,1)}, u32[]{:S(2)}) copy-start(bf16[64,6144]{1,0:T(8,128)(2,1)} %param.16) | copy-start | bytes 2359300
  268.7 14.2 %copy-start.6 = (u32[32]{0:T(128)S(1)}, u32[32]{0:T(128)}, u32[]{:S(2)}) copy-start(u32[32]{0:T(128)} %constant.31) | copy-start | bytes 388
Sparse Core Ops, SparseCore 0:
  165.8 91.0 all-reduce.3
  282.9 91.7 all-reduce.5
where the time goes:
time: 384 us
  waiting for transfers between devices  196 us (51%)
  blocking collectives  100 us (26%)
  matrix products  51.3 us (13%)
  between operations  13.6 us (4%)
  other arithmetic  8.77 us (2%)
  starting transfers between devices  7.26 us (2%)
  local copies, waits for them, and re-layouts  6.84 us (2%)
    unnamed x3, waiting for transfers between devices  91.3 us
    psum x1, waiting for transfers between devices, local(): first_all = lax.psum(partial_all, 'tensor')  91 us
    all_gather x3, blocking collectives, spread_rows(): lax.all_gather(local_rows, 'tensor', axis=0, tiled=True)  61.8 us
    all_gather x1, blocking collectives, local(): value_piece = lax.all_gather(value_rows, 'tensor', axis=0, tiled=True)  19.6 us
    all_gather x1, blocking collectives, local(): key_piece = lax.all_gather(key_rows, 'tensor', axis=0, tiled=True)  18.8 us
    dot_general x2, matrix products, local_hidden(): jnp.einsum('pmd,dc->pmc', normed, gate_mat, preferred_element_type=jnp.fl...  13.7 us
    all_to_all x2, waiting for transfers between devices, to_tokens(): lax.all_to_all(columns, 'tensor', split_axis=0, concat_axis=2, tiled=True)  13.3 us
    dot_general x1, matrix products, down_sum(): jnp.einsum('pmc,cd->pmd', hidden_all, down_mat, preferred_element_type=jn...  12.6 us
  transfers between devices with their start and end apart: 4, of which 4 were waited for; matrix products, arithmetic and copies ran while one was open for 0% of the time, Pallas kernels for 0%

commit v1 on v0

--- a/solution.py
+++ b/solution.py
@@ -5,6 +5,27 @@
 
 H = 48
 HD = 128
+
+
+def collect(shard, axis, dim):
+    peers, index, extent = (lax.axis_size(axis), lax.axis_index(axis), shard.shape[dim])
+    upward = [(i, (i + 1) % peers) for i in range(peers)]
+    left = [(i, (i - 1) % peers) for i in range(peers)]
+    result = jnp.zeros((*shard.shape[:dim], peers * extent, *shard.shape[dim + 1 :]), shard.dtype)
+    result = lax.dynamic_update_slice_in_dim(result, shard, index * extent, axis=dim)
+    from_left = from_right = shard
+    halfway = peers // 2
+    for hop in range(1, halfway + 1):
+        from_left = lax.ppermute(from_left, axis, upward)
+        result = lax.dynamic_update_slice_in_dim(
+            result, from_left, (index - hop) % peers * extent, axis=dim
+        )
+        if hop < peers - halfway:
+            from_right = lax.ppermute(from_right, axis, left)
+            result = lax.dynamic_update_slice_in_dim(
+                result, from_right, (index + hop) % peers * extent, axis=dim
+            )
+    return result
 
 
 def norm_rows(values, gain_vec):
@@ -73,7 +94,7 @@
     value_rows = projected[..., 2 * feat_width :]
     score_scale = HD ** (-0.5)
     key_piece = lax.all_gather(key_rows, "tensor", axis=0, tiled=True)
-    value_piece = lax.all_gather(value_rows, "tensor", axis=0, tiled=True)
+    value_piece = collect(value_rows, "tensor", 0)
     piece_rows = key_piece.shape[0]
     key_heads = key_piece.reshape(piece_rows, micro_count, H, HD)
     value_heads = value_piece.reshape(piece_rows, micro_count, H, HD)

time: 384 us -> 409 us (1.065)
  starting transfers between devices: 7.26 us -> 34.9 us
  blocking collectives: 100 us -> 89.4 us
  waiting for transfers between devices: 196 us -> 203 us
    ppermute x0 -> x15, starting transfers between devices: none -> 31.1 us  [the longest x7 30.7 us: collect(): from_right = lax.ppermute(from_right, axis, left)]
    all_gather x1 -> x0, blocking collectives: 19.6 us -> none  [local(): value_piece = lax.all_gather(value_rows, 'tensor', axis=0, tiled=True)]
    ppermute x0 -> x15, waiting for transfers between devices: none -> 14.6 us  [the longest x8 14.5 us: collect(): from_left = lax.ppermute(from_left, axis, upward)]
    all_to_all x0 -> x1, blocking collectives: none -> 9.95 us  [to_tokens(): lax.all_to_all(columns, 'tensor', split_axis=0, concat_axis=2, tiled=True)]
    all_to_all x2 -> x1, waiting for transfers between devices: 13.3 us -> 6.52 us  [to_tokens(): lax.all_to_all(columns, 'tensor', split_axis=0, concat_axis=2, tiled=True)]
  transfers between devices with their start and end apart: 4 -> 18, of which waited for: 4 -> 10; matrix products, arithmetic and copies ran while one was open for 0% -> 0% of each run, Pallas kernels for 0% -> 0%
where the time goes in v1:
time: 409 us
  waiting for transfers between devices  203 us (50%)
  blocking collectives  89.4 us (22%)
  matrix products  51.3 us (13%)
  starting transfers between devices  34.9 us (9%)
  between operations  13.9 us (3%)
  other arithmetic  8.84 us (2%)
  local copies, waits for them, and re-layouts  6.96 us (2%)
    unnamed x3, waiting for transfers between devices  91.3 us
    psum x1, waiting for transfers between devices, local(): first_all = lax.psum(partial_all, 'tensor')  90.9 us
    all_gather x3, blocking collectives, spread_rows(): lax.all_gather(local_rows, 'tensor', axis=0, tiled=True)  61.2 us
    ppermute x7, starting transfers between devices, collect(): from_right = lax.ppermute(from_right, axis, left)  30.7 us
    all_gather x1, blocking collectives, local(): key_piece = lax.all_gather(key_rows, 'tensor', axis=0, tiled=True)  18.2 us
    ppermute x8, waiting for transfers between devices, collect(): from_left = lax.ppermute(from_left, axis, upward)  14.5 us
    dot_general x2, matrix products, local_hidden(): jnp.einsum('pmd,dc->pmc', normed, gate_mat, preferred_element_type=jnp.fl...  13.7 us
    dot_general x1, matrix products, down_sum(): jnp.einsum('pmc,cd->pmd', hidden_all, down_mat, preferred_element_type=jn...  12.6 us
  transfers between devices with their start and end apart: 18, of which 10 were waited for; matrix products, arithmetic and copies ran while one was open for 0% of the time, Pallas kernels for 0%

profile of v1, /device:TPU:0, one launch (start us, length us, event | category | flops | bytes accessed | tf_op | source)
XLA Modules:
  0.0 408.6 jit_solution(6879594087325261260)
XLA Ops:
  6.5 1.1 copy-done
  7.7 1.0 fusion.79
  8.7 0.2 multiply_reduce_fusion.2
  9.0 0.8 fusion.64
  9.8 24.2 %all-gather.2 = bf16[16,2,6144]{2,1,0:T(2,128)(2,1)S(1)} all-gather(bf16[1,2,6144]{2,1,0:T(2,128)(2,1)S(1)} %fusion.64), channel_id=2, replica_groups=mesh['groups'=2,'tensor'=16] {'tensor'}, dimensions={0}, use_global_device_ids=true | all-gather | bytes 417792 | tf_op jit(solution)/shard_map/all_gather | solution.py:45
  34.0 7.6 %fusion.16 = bf16[16,2,1152]{2,0,1:T(8,128)(2,1)S(1)} fusion(bf16[6144,1152]{1,0:T(8,128)(2,1)} %param.18, bf16[16,2,6144]{2,1,0:T(2,128)(2,1)S(1)} %all-gather.2), kind=kOutput, calls=%fused_computation.16 | convolution fusion | flops 453021696 | bytes 14622720 | tf_op jit(solution)/shard_map/pmd,dc->pmc/dot_general | solution.py:86
  41.6 0.7 copy.49
  42.2 3.5 all-to-all-start
  46.2 6.5 %all-to-all-done = bf16[16,2,1152]{2,1,0:T(2,128)(2,1)S(1)} async-done(((bf16[16,2,1152]{2,1,0:T(2,128)(2,1)}), bf16[16,2,1152]{2,1,0:T(2,128)(2,1)S(1)}, u32[]{:S(2)}, u32[]{:S(2)}) %all-to-all-start) | async-done | bytes 73760 | tf_op jit(solution)/shard_map/all_to_all | solution.py:49
  53.0 4.4 %collective-permute-start.1 = (bf16[1,2,6144]{2,1,0:T(2,128)(2,1)S(1)}, bf16[1,2,6144]{2,1,0:T(2,128)(2,1)S(1)}, u32[]{:S(2)}, u32[]{:S(2)}) collective-permute-start(bf16[1,2,6144]{2,1,0:T(2,128)(2,1)S(1)} %get-tuple-element.7), channel_id=1, source_target_pairs={{0,15},{1,0},{2,1},{3,2},{4,3},{5,4},{6,5},{7,6},{8,7},{9,8},{10,9... | collective-permute-start | bytes 73736 | tf_op jit(solution)/shard_map/ppermute | solution.py:24
  57.5 18.2 %all_gather.13 = bf16[16,2,6144]{2,1,0:T(2,128)(2,1)S(1)} all-gather(bf16[1,2,6144]{2,1,0:T(2,128)(2,1)S(1)} %get-tuple-element.10), channel_id=1, replica_groups=mesh['groups'=2,'tensor'=16] {'tensor'}, dimensions={0}, use_global_device_ids=true | all-gather | bytes 417792 | tf_op jit(solution)/shard_map/all_gather | solution.py:96
  75.7 0.2 reshape.163
  76.0 0.3 fusion.40
  76.6 0.4 collective-permute-start.2
  77.0 4.1 %collective-permute-start.3 = (bf16[1,2,6144]{2,1,0:T(2,128)(2,1)S(1)}, bf16[1,2,6144]{2,1,0:T(2,128)(2,1)S(1)}, u32[]{:S(2)}, u32[]{:S(2)}) collective-permute-start(bf16[1,2,6144]{2,1,0:T(2,128)(2,1)S(1)} %collective-permute-done.1), channel_id=1, source_target_pairs={{0,15},{1,0},{2,1},{3,2},{4,3},{5,4},{6,5},{7,6},{8,7},{9,8},{10,9... | collective-permute-start | bytes 73736 | tf_op jit(solution)/shard_map/ppermute | solution.py:24
  81.2 1.4 collective-permute-done.2
  82.6 4.4 %collective-permute-start.5 = (bf16[1,2,6144]{2,1,0:T(2,128)(2,1)S(1)}, bf16[1,2,6144]{2,1,0:T(2,128)(2,1)S(1)}, u32[]{:S(2)}, u32[]{:S(2)}) collective-permute-start(bf16[1,2,6144]{2,1,0:T(2,128)(2,1)S(1)} %collective-permute-done.3), channel_id=1, source_target_pairs={{0,15},{1,0},{2,1},{3,2},{4,3},{5,4},{6,5},{7,6},{8,7},{9,8},{10,9... | collective-permute-start | bytes 73736 | tf_op jit(solution)/shard_map/ppermute | solution.py:24
  87.1 1.4 collective-permute-done.4
  88.6 4.4 %collective-permute-start.7 = (bf16[1,2,6144]{2,1,0:T(2,128)(2,1)S(1)}, bf16[1,2,6144]{2,1,0:T(2,128)(2,1)S(1)}, u32[]{:S(2)}, u32[]{:S(2)}) collective-permute-start(bf16[1,2,6144]{2,1,0:T(2,128)(2,1)S(1)} %collective-permute-done.5), channel_id=1, source_target_pairs={{0,15},{1,0},{2,1},{3,2},{4,3},{5,4},{6,5},{7,6},{8,7},{9,8},{10,9... | collective-permute-start | bytes 73736 | tf_op jit(solution)/shard_map/ppermute | solution.py:24
  93.1 1.4 collective-permute-done.6
  94.5 4.4 %collective-permute-start.9 = (bf16[1,2,6144]{2,1,0:T(2,128)(2,1)S(1)}, bf16[1,2,6144]{2,1,0:T(2,128)(2,1)S(1)}, u32[]{:S(2)}, u32[]{:S(2)}) collective-permute-start(bf16[1,2,6144]{2,1,0:T(2,128)(2,1)S(1)} %collective-permute-done.7), channel_id=1, source_target_pairs={{0,15},{1,0},{2,1},{3,2},{4,3},{5,4},{6,5},{7,6},{8,7},{9,8},{10,9... | collective-permute-start | bytes 73736 | tf_op jit(solution)/shard_map/ppermute | solution.py:24
  99.0 1.4 collective-permute-done.8
  100.5 4.4 %collective-permute-start.11 = (bf16[1,2,6144]{2,1,0:T(2,128)(2,1)S(1)}, bf16[1,2,6144]{2,1,0:T(2,128)(2,1)S(1)}, u32[]{:S(2)}, u32[]{:S(2)}) collective-permute-start(bf16[1,2,6144]{2,1,0:T(2,128)(2,1)S(1)} %collective-permute-done.9), channel_id=1, source_target_pairs={{0,15},{1,0},{2,1},{3,2},{4,3},{5,4},{6,5},{7,6},{8,7},{9,8},{10,9... | collective-permute-start | bytes 73736 | tf_op jit(solution)/shard_map/ppermute | solution.py:24
  105.0 1.4 collective-permute-done.10
  106.4 4.4 %collective-permute-start.13 = (bf16[1,2,6144]{2,1,0:T(2,128)(2,1)S(1)}, bf16[1,2,6144]{2,1,0:T(2,128)(2,1)S(1)}, u32[]{:S(2)}, u32[]{:S(2)}) collective-permute-start(bf16[1,2,6144]{2,1,0:T(2,128)(2,1)S(1)} %collective-permute-done.11), channel_id=1, source_target_pairs={{0,15},{1,0},{2,1},{3,2},{4,3},{5,4},{6,5},{7,6},{8,7},{9,8},{10,9... | collective-permute-start | bytes 73736 | tf_op jit(solution)/shard_map/ppermute | solution.py:24
  110.9 1.4 collective-permute-done.12
  112.4 5.9 %collective-permute-done.14 = bf16[1,2,6144]{2,1,0:T(2,128)(2,1)S(1)} collective-permute-done((bf16[1,2,6144]{2,1,0:T(2,128)(2,1)S(1)}, bf16[1,2,6144]{2,1,0:T(2,128)(2,1)S(1)}, u32[]{:S(2)}, u32[]{:S(2)}) %collective-permute-start.14) | collective-permute-done | bytes 24608 | tf_op jit(solution)/shard_map/ppermute | solution.py:19
  118.3 0.2 reshape.162
  118.6 0.2 fusion.38
  119.0 18.3 %all_gather.14 = bf16[16,2,6144]{2,1,0:T(2,128)(2,1)S(1)} all-gather(bf16[1,2,6144]{2,1,0:T(2,128)(2,1)S(1)} %convert_element_type.75), channel_id=1, replica_groups=mesh['groups'=2,'tensor'=16] {'tensor'}, dimensions={0}, use_global_device_ids=true | all-gather | bytes 417792 | tf_op jit(solution)/shard_map/all_gather | solution.py:45
  137.2 3.1 fusion.35
  140.4 10.0 %all_to_all.27 = bf16[16,2,384]{2,1,0:T(2,128)(2,1)S(1)} all-to-all(bf16[16,2,384]{2,1,0:T(2,128)(2,1)S(1)} %copy.51), channel_id=1, replica_groups=mesh['groups'=2,'tensor'=16] {'tensor'}, dimensions={0} | all-to-all | bytes 49152 | tf_op jit(solution)/shard_map/all_to_all | solution.py:49
  150.9 18.8 %all-gather.3 = bf16[16,2,6144]{2,1,0:T(2,128)(2,1)S(1)} all-gather(bf16[1,2,6144]{2,1,0:T(2,128)(2,1)S(1)} %fusion.65), channel_id=3, replica_groups=mesh['groups'=2,'tensor'=16] {'tensor'}, dimensions={0}, use_global_device_ids=true | all-gather | bytes 417792 | tf_op jit(solution)/shard_map/all_gather | solution.py:45
  169.7 6.8 %fusion.12 = f32[16,2,1024]{2,0,1:T(8,128)S(1)} fusion(bf16[6144,1024]{1,0:T(8,128)(2,1)} %param.21, bf16[16,2,6144]{2,1,0:T(2,128)(2,1)S(1)} %all-gather.3), kind=kOutput, calls=%fused_computation.12 | convolution fusion | flops 402653184 | bytes 13107200 | tf_op jit(solution)/shard_map/pmd,dc->pmc/dot_general | solution.py:39
  176.6 12.6 %fusion.8 = f32[16,2,6144]{2,0,1:T(8,128)S(1)} fusion(bf16[1024,6144]{1,0:T(8,128)(2,1)} %param.23, bf16[6144,1024]{1,0:T(8,128)(2,1)} %param.22, bf16[16,2,6144]{2,1,0:T(2,128)(2,1)S(1)} %all-gather.3, f32[16,2,1024]{2,0,1:T(8,128)S(1)} %fusion.12), kind=kOutput, calls=%fused_computation.8 | convolution fusion | flops 805502976 | bytes 26476544 | tf_op jit(solution)/shard_map/pmc,cd->pmd/dot_general | solution.py:133
  189.2 0.6 copy.55
  189.9 0.9 copy-done.2
  190.8 0.3 all-reduce.6.cloned.1.call-start
  191.1 90.9 %all-reduce.4.cloned.1.call-done = f32[16,2,6144]{2,1,0:T(2,128)} async-done(((f32[16,2,6144]{2,1,0:T(2,128)}), f32[16,2,6144]{2,1,0:T(2,128)}) %all-reduce.4.cloned.1.call-update) | async-done | bytes 786448 | tf_op jit(solution)/shard_map/psum | solution.py:138
  281.9 1.4 reduce_sum.68
  283.4 1.7 multiply_reduce_fusion
  285.1 1.7 multiply_convert_fusion
  286.8 6.9 %fusion.6 = f32[16,2,1024]{2,0,1:T(8,128)S(1)} fusion(bf16[6144,1024]{1,0:T(8,128)(2,1)} %param.25, bf16[16,2,6144]{2,1,0:T(2,128)(2,1)S(1)} %multiply_convert_fusion), kind=kOutput, calls=%fused_computation.6 | convolution fusion | flops 402653184 | bytes 13107200 | tf_op jit(solution)/shard_map/pmd,dc->pmc/dot_general | solution.py:39
  293.7 12.6 %fusion.2 = f32[16,2,6144]{2,0,1:T(8,128)S(1)} fusion(bf16[1024,6144]{1,0:T(8,128)(2,1)} %param.27, bf16[6144,1024]{1,0:T(8,128)(2,1)} %param.26, bf16[16,2,6144]{2,1,0:T(2,128)(2,1)S(1)} %multiply_convert_fusion, f32[16,2,1024]{2,0,1:T(8,128)S(1)} %fusion.6), kind=kOutput, calls=%fused_computation.2 | convolution fusion | flops 805502976 | bytes 26476544 | tf_op jit(solution)/shard_map/pmc,cd->pmd/dot_general | solution.py:54
  306.3 1.5 copy.58
  307.8 0.6 dynamic-slice
  308.5 91.2 %all-reduce.6.cloned.1.call-done = f32[16,2,6144]{2,1,0:T(2,128)} async-done(((f32[16,2,6144]{2,1,0:T(2,128)}), f32[16,2,6144]{2,1,0:T(2,128)}) %all-reduce.6.cloned.1.call-update) | async-done | bytes 786448
  399.7 2.1 fusion.62
  (66 shorter events, 2.1 us)
Async XLA Ops:
  6.5 1.1 copy-start
  6.5 39.6 %copy-start.5 = (s32[2]{0:T(128)S(1)}, s32[2]{0:T(128)}, u32[]{:S(2)}) copy-start(s32[2]{0:T(128)} %param.15) | copy-start | bytes 28
  34.0 116.8 %copy-start.3 = (f32[6144]{0:T(1024)S(1)}, f32[6144]{0:T(1024)}, u32[]{:S(2)}) copy-start(f32[6144]{0:T(1024)} %param.20) | copy-start | bytes 73732
  42.2 10.5 %all-to-all-start = ((bf16[16,2,1152]{2,1,0:T(2,128)(2,1)}), bf16[16,2,1152]{2,1,0:T(2,128)(2,1)S(1)}, u32[]{:S(2)}, u32[]{:S(2)}) async-start(bf16[16,2,1152]{2,1,0:T(2,128)(2,1)} %copy.49), calls=%async_computation | async-start | bytes 147456 | tf_op jit(solution)/shard_map/all_to_all | solution.py:49
  45.7 236.2 %all-reduce.4.cloned.1.call-start = ((), (), s32[]{:S(2)}) async-start(), calls=%async_computation.2 | async-start | bytes 1572864 | tf_op jit(solution)/shard_map/psum | solution.py:138
  53.0 23.6 %collective-permute-start = (bf16[1,2,6144]{2,1,0:T(2,128)(2,1)S(1)}, bf16[1,2,6144]{2,1,0:T(2,128)(2,1)S(1)}, u32[]{:S(2)}, u32[]{:S(2)}) collective-permute-start(bf16[1,2,6144]{2,1,0:T(2,128)(2,1)S(1)} %get-tuple-element.7), channel_id=1, source_target_pairs={{0,1},{1,2},{2,3},{3,4},{4,5},{5,6},{6,7},{7,8},{8,9},{9,10},{10,1... | collective-permute-start | bytes 73736 | tf_op jit(solution)/shard_map/ppermute | solution.py:19
  53.0 24.0 %collective-permute-start.1 = (bf16[1,2,6144]{2,1,0:T(2,128)(2,1)S(1)}, bf16[1,2,6144]{2,1,0:T(2,128)(2,1)S(1)}, u32[]{:S(2)}, u32[]{:S(2)}) collective-permute-start(bf16[1,2,6144]{2,1,0:T(2,128)(2,1)S(1)} %get-tuple-element.7), channel_id=1, source_target_pairs={{0,15},{1,0},{2,1},{3,2},{4,3},{5,4},{6,5},{7,6},{8,7},{9,8},{10,9... | collective-permute-start | bytes 73736 | tf_op jit(solution)/shard_map/ppermute | solution.py:24
  76.6 6.0 %collective-permute-start.2 = (bf16[1,2,6144]{2,1,0:T(2,128)(2,1)S(1)}, bf16[1,2,6144]{2,1,0:T(2,128)(2,1)S(1)}, u32[]{:S(2)}, u32[]{:S(2)}) collective-permute-start(bf16[1,2,6144]{2,1,0:T(2,128)(2,1)S(1)} %collective-permute-done), channel_id=1, source_target_pairs={{0,1},{1,2},{2,3},{3,4},{4,5},{5,6},{6,7},{7,8},{8,9},{9,10},{10,1... | collective-permute-start | bytes 73736 | tf_op jit(solution)/shard_map/ppermute | solution.py:19
  77.0 5.6 %collective-permute-start.3 = (bf16[1,2,6144]{2,1,0:T(2,128)(2,1)S(1)}, bf16[1,2,6144]{2,1,0:T(2,128)(2,1)S(1)}, u32[]{:S(2)}, u32[]{:S(2)}) collective-permute-start(bf16[1,2,6144]{2,1,0:T(2,128)(2,1)S(1)} %collective-permute-done.1), channel_id=1, source_target_pairs={{0,15},{1,0},{2,1},{3,2},{4,3},{5,4},{6,5},{7,6},{8,7},{9,8},{10,9... | collective-permute-start | bytes 73736 | tf_op jit(solution)/shard_map/ppermute | solution.py:24
  82.6 5.9 %collective-permute-start.4 = (bf16[1,2,6144]{2,1,0:T(2,128)(2,1)S(1)}, bf16[1,2,6144]{2,1,0:T(2,128)(2,1)S(1)}, u32[]{:S(2)}, u32[]{:S(2)}) collective-permute-start(bf16[1,2,6144]{2,1,0:T(2,128)(2,1)S(1)} %collective-permute-done.2), channel_id=1, source_target_pairs={{0,1},{1,2},{2,3},{3,4},{4,5},{5,6},{6,7},{7,8},{8,9},{9,10},{10,1... | collective-permute-start | bytes 73736 | tf_op jit(solution)/shard_map/ppermute | solution.py:19
  82.6 5.9 %collective-permute-start.5 = (bf16[1,2,6144]{2,1,0:T(2,128)(2,1)S(1)}, bf16[1,2,6144]{2,1,0:T(2,128)(2,1)S(1)}, u32[]{:S(2)}, u32[]{:S(2)}) collective-permute-start(bf16[1,2,6144]{2,1,0:T(2,128)(2,1)S(1)} %collective-permute-done.3), channel_id=1, source_target_pairs={{0,15},{1,0},{2,1},{3,2},{4,3},{5,4},{6,5},{7,6},{8,7},{9,8},{10,9... | collective-permute-start | bytes 73736 | tf_op jit(solution)/shard_map/ppermute | solution.py:24
  88.5 5.9 %collective-permute-start.6 = (bf16[1,2,6144]{2,1,0:T(2,128)(2,1)S(1)}, bf16[1,2,6144]{2,1,0:T(2,128)(2,1)S(1)}, u32[]{:S(2)}, u32[]{:S(2)}) collective-permute-start(bf16[1,2,6144]{2,1,0:T(2,128)(2,1)S(1)} %collective-permute-done.4), channel_id=1, source_target_pairs={{0,1},{1,2},{2,3},{3,4},{4,5},{5,6},{6,7},{7,8},{8,9},{9,10},{10,1... | collective-permute-start | bytes 73736 | tf_op jit(solution)/shard_map/ppermute | solution.py:19
  88.6 5.9 %collective-permute-start.7 = (bf16[1,2,6144]{2,1,0:T(2,128)(2,1)S(1)}, bf16[1,2,6144]{2,1,0:T(2,128)(2,1)S(1)}, u32[]{:S(2)}, u32[]{:S(2)}) collective-permute-start(bf16[1,2,6144]{2,1,0:T(2,128)(2,1)S(1)} %collective-permute-done.5), channel_id=1, source_target_pairs={{0,15},{1,0},{2,1},{3,2},{4,3},{5,4},{6,5},{7,6},{8,7},{9,8},{10,9... | collective-permute-start | bytes 73736 | tf_op jit(solution)/shard_map/ppermute | solution.py:24
  94.5 5.9 %collective-permute-start.8 = (bf16[1,2,6144]{2,1,0:T(2,128)(2,1)S(1)}, bf16[1,2,6144]{2,1,0:T(2,128)(2,1)S(1)}, u32[]{:S(2)}, u32[]{:S(2)}) collective-permute-start(bf16[1,2,6144]{2,1,0:T(2,128)(2,1)S(1)} %collective-permute-done.6), channel_id=1, source_target_pairs={{0,1},{1,2},{2,3},{3,4},{4,5},{5,6},{6,7},{7,8},{8,9},{9,10},{10,1... | collective-permute-start | bytes 73736 | tf_op jit(solution)/shard_map/ppermute | solution.py:19
  94.5 5.9 %collective-permute-start.9 = (bf16[1,2,6144]{2,1,0:T(2,128)(2,1)S(1)}, bf16[1,2,6144]{2,1,0:T(2,128)(2,1)S(1)}, u32[]{:S(2)}, u32[]{:S(2)}) collective-permute-start(bf16[1,2,6144]{2,1,0:T(2,128)(2,1)S(1)} %collective-permute-done.7), channel_id=1, source_target_pairs={{0,15},{1,0},{2,1},{3,2},{4,3},{5,4},{6,5},{7,6},{8,7},{9,8},{10,9... | collective-permute-start | bytes 73736 | tf_op jit(solution)/shard_map/ppermute | solution.py:24
  100.4 5.9 %collective-permute-start.10 = (bf16[1,2,6144]{2,1,0:T(2,128)(2,1)S(1)}, bf16[1,2,6144]{2,1,0:T(2,128)(2,1)S(1)}, u32[]{:S(2)}, u32[]{:S(2)}) collective-permute-start(bf16[1,2,6144]{2,1,0:T(2,128)(2,1)S(1)} %collective-permute-done.8), channel_id=1, source_target_pairs={{0,1},{1,2},{2,3},{3,4},{4,5},{5,6},{6,7},{7,8},{8,9},{9,10},{10,1... | collective-permute-start | bytes 73736 | tf_op jit(solution)/shard_map/ppermute | solution.py:19
  100.5 5.9 %collective-permute-start.11 = (bf16[1,2,6144]{2,1,0:T(2,128)(2,1)S(1)}, bf16[1,2,6144]{2,1,0:T(2,128)(2,1)S(1)}, u32[]{:S(2)}, u32[]{:S(2)}) collective-permute-start(bf16[1,2,6144]{2,1,0:T(2,128)(2,1)S(1)} %collective-permute-done.9), channel_id=1, source_target_pairs={{0,15},{1,0},{2,1},{3,2},{4,3},{5,4},{6,5},{7,6},{8,7},{9,8},{10,9... | collective-permute-start | bytes 73736 | tf_op jit(solution)/shard_map/ppermute | solution.py:24
  106.4 5.9 %collective-permute-start.12 = (bf16[1,2,6144]{2,1,0:T(2,128)(2,1)S(1)}, bf16[1,2,6144]{2,1,0:T(2,128)(2,1)S(1)}, u32[]{:S(2)}, u32[]{:S(2)}) collective-permute-start(bf16[1,2,6144]{2,1,0:T(2,128)(2,1)S(1)} %collective-permute-done.10), channel_id=1, source_target_pairs={{0,1},{1,2},{2,3},{3,4},{4,5},{5,6},{6,7},{7,8},{8,9},{9,10},{10,1... | collective-permute-start | bytes 73736 | tf_op jit(solution)/shard_map/ppermute | solution.py:19
  106.4 6.0 %collective-permute-start.13 = (bf16[1,2,6144]{2,1,0:T(2,128)(2,1)S(1)}, bf16[1,2,6144]{2,1,0:T(2,128)(2,1)S(1)}, u32[]{:S(2)}, u32[]{:S(2)}) collective-permute-start(bf16[1,2,6144]{2,1,0:T(2,128)(2,1)S(1)} %collective-permute-done.11), channel_id=1, source_target_pairs={{0,15},{1,0},{2,1},{3,2},{4,3},{5,4},{6,5},{7,6},{8,7},{9,8},{10,9... | collective-permute-start | bytes 73736 | tf_op jit(solution)/shard_map/ppermute | solution.py:24
  112.3 5.9 %collective-permute-start.14 = (bf16[1,2,6144]{2,1,0:T(2,128)(2,1)S(1)}, bf16[1,2,6144]{2,1,0:T(2,128)(2,1)S(1)}, u32[]{:S(2)}, u32[]{:S(2)}) collective-permute-start(bf16[1,2,6144]{2,1,0:T(2,128)(2,1)S(1)} %collective-permute-done.12), channel_id=1, source_target_pairs={{0,1},{1,2},{2,3},{3,4},{4,5},{5,6},{6,7},{7,8},{8,9},{9,10},{10,1... | collective-permute-start | bytes 73736 | tf_op jit(solution)/shard_map/ppermute | solution.py:19
  176.6 108.5 %copy-start.4 = (f32[6144]{0:T(1024)S(1)}, f32[6144]{0:T(1024)}, u32[]{:S(2)}) copy-start(f32[6144]{0:T(1024)} %param.24) | copy-start | bytes 73732
  189.9 0.9 copy-start.2
  190.8 208.9 %all-reduce.6.cloned.1.call-start = ((), (), s32[]{:S(2)}) async-start(), calls=%async_computation.3 | async-start | bytes 1572864
  286.7 115.0 %copy-start.1 = (bf16[64,6144]{1,0:T(8,128)(2,1)S(1)}, bf16[64,6144]{1,0:T(8,128)(2,1)}, u32[]{:S(2)}) copy-start(bf16[64,6144]{1,0:T(8,128)(2,1)} %param.16) | copy-start | bytes 2359300
  293.7 14.2 %copy-start.6 = (u32[32]{0:T(128)S(1)}, u32[32]{0:T(128)}, u32[]{:S(2)}) copy-start(u32[32]{0:T(128)} %constant.130) | copy-start | bytes 388
Sparse Core Ops, SparseCore 0:
  190.9 90.9 all-reduce.3
  307.9 91.7 all-reduce.5
